TPU v7x, 256 devices: a whole 4x4x8 slice. The times are simulated.
256 devices in a mesh: dp: 8 (over y, x_hi), proto: 16 (over z, core), crop: 2 (over x_lo).
Axes of the slice: x: 4 (x_hi: 2, x_lo: 2; x = x_hi * 2 + x_lo), y: 4, z: 8, core: 2. Of those that a mesh axis runs over, the one named last changes fastest.
Arguments:
- embeddings: bfloat16 [2048, 2, 4, 256], P(('dp', 'proto'), 'crop'), may hold values from -2 to 2
- codes: bfloat16 [2048, 2, 65536], P('dp', 'crop', 'proto'), may hold values from 0 to 1, as said below
- prototypes: bfloat16 [16, 4096, 256], P('proto', ('dp', 'crop')), may hold values from -2 to 2
Outputs:
- grad_emb: float32 [2048, 2, 4, 256], P(('dp', 'proto'), 'crop')
- grad_proto: float32 [16, 4096, 256], P('proto', ('dp', 'crop'))
Inputs may be any that keep to these rules, and one draw needn't show every extreme that they name: `codes`: each image's code is a distribution over the prototypes: nonnegative entries that sum to about one over all 65536.
All inputs are finite; a program needn't handle non-finite values.
Results may differ from a plain program's by a relative error of at most 0.0031.
Values may be sent and summed in bfloat16 or wider, within the bound.
No kernel may reach another device: no remote copies, remote signals or barrier semaphores. Data moves between devices by JAX's collectives and lax.ppermute only.
A program may use at most 64 MiB of HBM per device.

v0:
```python
import jax
import jax.numpy as jnp
from jax import lax
from jax.sharding import PartitionSpec as P

sharpness_divisor = 0.1
epsilon = 1e-06


def swapped(value, axis, distance):
    mask = 2**distance
    pairs = [(source, source ^ mask) for source in range(lax.axis_size(axis))]
    return lax.ppermute(value, axis, pairs)


def normalize_rows(values):
    floats = values.astype(jnp.float32)
    lengths = jnp.sqrt(jnp.sum(floats * floats, axis=-1, keepdims=True) + epsilon)
    return (floats / lengths, lengths)


def contract_first(left, right):
    return lax.dot_general(
        left, right, (((0,), (0,)), ((), ())), preferred_element_type=jnp.float32
    )


def on_device(embeddings, codes, prototypes):
    unit_emb, emb_norm = normalize_rows(embeddings)
    rounded = unit_emb.astype(jnp.bfloat16)
    unit_proto, proto_norm = normalize_rows(prototypes[0])
    rescaled_input = lax.all_gather(
        unit_proto.astype(jnp.bfloat16), ("dp", "crop"), axis=0, tiled=True
    )
    gathered = lax.all_gather(rounded, "proto", axis=0, tiled=True)
    images = gathered.shape[0]
    crop_count = gathered.shape[2]
    features = gathered.shape[3]
    as_floats = gathered[:, 0].astype(jnp.float32)
    local_sum = jnp.sum(as_floats[:, 1:], axis=1)
    outgoing = as_floats[:, 0] + local_sum
    own_code = codes[:, 0]
    own_term = jnp.dot(own_code, rescaled_input, preferred_element_type=jnp.float32)
    incoming = swapped(outgoing, "crop", 0)
    partner_code = swapped(own_code, "crop", 0)
    other_term = jnp.dot(partner_code, rescaled_input, preferred_element_type=jnp.float32)
    target_sum = (local_sum + incoming).astype(jnp.bfloat16)
    view_results = jnp.where(jnp.arange(crop_count) == 0, 1.0, 2.0).astype(jnp.float32)
    block_images = min(images, 128)
    blocks = images // block_images
    row_blocks = gathered.reshape(blocks, block_images * crop_count, features)

    def block_exponent(row_block):
        prototype_scores = lax.dot_general(
            row_block, rescaled_input, (((1,), (1,)), ((), ())), preferred_element_type=jnp.float32
        )
        return jnp.exp(prototype_scores / sharpness_divisor)

    partial_totals = lax.map(
        lambda row_block: jnp.sum(block_exponent(row_block), axis=1), row_blocks
    )
    totals = lax.psum(partial_totals, "proto")
    row_weight = jnp.tile(view_results, block_images)[:, None]

    def backward_block(running, inputs):
        row_block, block_total = inputs
        probs = (block_exponent(row_block) / block_total[:, None]).astype(jnp.bfloat16)
        softened_rows = jnp.dot(probs, rescaled_input, preferred_element_type=jnp.float32)
        weighted = (row_block.astype(jnp.float32) * row_weight).astype(jnp.bfloat16)
        return (running + contract_first(probs, weighted), softened_rows)

    start_sum = jnp.zeros((rescaled_input.shape[0], features), jnp.float32)
    proto_sum, softened_rows = lax.scan(backward_block, start_sum, (row_blocks, totals))
    proto_sum = proto_sum - contract_first(own_code, target_sum)
    softened_rows = softened_rows.reshape(images, crop_count, features)
    is_global = (jnp.arange(crop_count) == 0)[None, :, None]
    assigned_code = jnp.where(
        is_global, other_term[:, None, :], (own_term + other_term)[:, None, :]
    )
    row_contributions = (
        softened_rows * view_results[None, :, None] - assigned_code
    ) / sharpness_divisor
    score_grad = lax.psum_scatter(row_contributions, "proto", scatter_dimension=0, tiled=True)[
        :, None
    ]
    grad_emb = (
        score_grad - unit_emb * jnp.sum(unit_emb * score_grad, axis=-1, keepdims=True)
    ) / emb_norm
    proto_grad = lax.psum_scatter(proto_sum, ("dp", "crop"), scatter_dimension=0, tiled=True)
    grad_proto = (
        proto_grad - unit_proto * jnp.sum(unit_proto * proto_grad, axis=-1, keepdims=True)
    ) / proto_norm
    return (grad_emb, grad_proto[None])


def solution(mesh):
    return jax.shard_map(
        on_device,
        mesh=mesh,
        in_specs=(
            P(("dp", "proto"), "crop", None, None),
            P("dp", "crop", "proto"),
            P("proto", ("dp", "crop"), None),
        ),
        out_specs=(P(("dp", "proto"), "crop", None, None), P("proto", ("dp", "crop"), None)),
        check_vma=False,
    )
```

profile of v0, /device:TPU:32, one launch (start us, length us, event | category | flops | bytes accessed | tf_op | source)
XLA Modules:
  0.0 344.7 jit_solution(12414158434441724650)
XLA Ops:
  9.6 1.6 collective-permute-start
  12.9 19.3 %all_gather.6 = bf16[256,1,4,256]{3,2,1,0:T(4,128)(2,1)S(1)} all-gather(bf16[16,1,4,256]{3,2,1,0:T(4,128)(2,1)S(1)} %fusion.20), channel_id=1, replica_groups=mesh['dp'=8,'proto'=16,'crop'=2] {'proto'}, dimensions={0}, use_global_device_ids=true | all-gather | bytes 557056 | tf_op jit(solution)/shard_map/all_gather | solution.py:35
  35.3 36.5 %all-gather.2.cloned.1.call-done = bf16[4096,256]{0,1:T(8,128)(2,1)} async-done(((bf16[256,256]{0,1:T(8,128)(2,1)}), bf16[4096,256]{0,1:T(8,128)(2,1)}) %all-gather.2.cloned.1.call-update) | async-done | bytes 2097168 | tf_op jit(solution)/shard_map/all_gather | solution.py:32
  71.8 4.1 %copy.21 = bf16[4096,256]{1,0:T(8,128)(2,1)} copy(bf16[4096,256]{0,1:T(8,128)(2,1)} %all-gather.2.cloned.1.call-done) | data formatting | bytes 4194304
  75.9 6.2 %while.23 = (s32[]{:T(128)}, f32[2,512]{1,0:T(2,128)S(1)}, bf16[2,512,256]{2,1,0:T(8,128)(2,1)S(1)}, bf16[4096,256]{1,0:T(8,128)(2,1)}, s32[]{:T(128)}, /*index=5*/s32[]{:T(128)}) while((s32[]{:T(128)}, f32[2,512]{1,0:T(2,128)S(1)}, bf16[2,512,256]{2,1,0:T(8,128)(2,1)S(1)}, bf16[4096,256]{1,0:T(8,128)(2,1)}, s32[]{:T(128)}, ...), condition=%wide.region_4.5_spmd, body=%wide.region_2.4_spmd.sunk | while | flops 1077935616 | bytes 2365525 | solution.py:59
  75.9 3.1 exponential_reduce_fusion.2
  79.1 3.0 exponential_reduce_fusion.2
  82.1 22.0 %psum.7 = f32[2,512]{1,0:T(2,128)S(1)} all-reduce(f32[2,512]{1,0:T(2,128)S(1)} %get-tuple-element.62), channel_id=1, replica_groups=mesh['dp'=8,'proto'=16,'crop'=2] {'proto'}, use_global_device_ids=true, to_apply=%region_5.6 | all-reduce | flops 1024 | bytes 8192 | tf_op jit(solution)/shard_map/psum | solution.py:62
  104.1 2.3 convolution_bitcast_fusion.3
  106.6 3.0 fusion.14
  110.7 19.1 %while.24 = (s32[]{:T(128)}, f32[4096,256]{1,0:T(8,128)}, f32[2,512,256]{2,1,0:T(8,128)}, bf16[2,512,256]{2,1,0:T(8,128)(2,1)S(1)}, bf16[4096,256]{1,0:T(8,128)(...) while((s32[]{:T(128)}, f32[4096,256]{1,0:T(8,128)}, ...), condition=%wide.region_7.8_spmd.clone, body=%wide.region_6.7_spmd.clone.sunk | while | flops 3230007296 | bytes 76560664 | solution.py:73
  110.9 3.5 %divide_convert_fusion.2 = bf16[512,4096]{1,0:T(8,128)(2,1)S(1)} fusion(bf16[4096,256]{1,0:T(8,128)(2,1)} %get-tuple-element.261, f32[512]{0:T(512)S(1)} %bitcast.87, bf16[2,512,256]{2,1,0:T(8,128)(2,1)S(1)} %get-tuple-element.260, s32[]{:T(128)S(6)} %copy.39), kind=kOutput, calls=%fused_computation.5.clone.1 | convolution fusion | flops 1080033280 | bytes 6555652 | tf_op jit(solution)/shard_map/while/body/eval_jaxpr/dot_general | solution.py:54
  116.6 1.7 convolution_add_fusion.2
  118.4 1.9 copy-done.1
  120.5 3.5 %divide_convert_fusion.2 = bf16[512,4096]{1,0:T(8,128)(2,1)S(1)} fusion(bf16[4096,256]{1,0:T(8,128)(2,1)} %get-tuple-element.261, f32[512]{0:T(512)S(1)} %bitcast.87, bf16[2,512,256]{2,1,0:T(8,128)(2,1)S(1)} %get-tuple-element.260, s32[]{:T(128)S(6)} %copy.39), kind=kOutput, calls=%fused_computation.5.clone.1 | convolution fusion | flops 1080033280 | bytes 6555652 | tf_op jit(solution)/shard_map/while/body/eval_jaxpr/dot_general | solution.py:54
  126.2 1.7 convolution_add_fusion.2
  127.9 1.9 copy-done.1
  129.9 1.5 reshape.54
  131.4 2.2 subtract_multiply_fusion
  133.7 5.8 %copy.24 = f32[4096,256]{0,1:T(8,128)} copy(f32[4096,256]{1,0:T(8,128)} %get-tuple-element.64) | data formatting | bytes 8388608 | tf_op jit(solution)/shard_map/while | solution.py:73
  139.5 5.0 %fusion.13 = f32[4096,256]{0,1:T(8,128)} fusion(f32[4096,256]{0,1:T(8,128)} %copy.24, f32[256,256]{1,0:T(8,128)S(1)} %slice_reduce_fusion, f32[256,256]{1,0:T(8,128)} %collective-permute-done.1, bf16[256,1,4096]{2,0,1:T(8,128)(2,1)S(1)} %copy-done.3), kind=kOutput, calls=%fused_computation.19 | convolution fusion | flops 538050560 | bytes 11010048 | tf_op jit(solution)/shard_map/dot_general | solution.py:23
  146.4 98.6 %all-reduce.3.cloned.1.call-done = f32[256,4,256]{2,1,0:T(4,128)} async-done(((f32[256,4,256]{2,1,0:T(4,128)}), f32[256,4,256]{2,1,0:T(4,128)}) %all-reduce.3.cloned.1.call-update) | async-done | bytes 1048592
  246.0 1.6 subtract_divide_fusion
  247.6 87.7 %reduce-scatter.2.cloned.1.call-done = f32[256,256]{0,1:T(8,128)} async-done(((f32[4096,256]{0,1:T(8,128)}), f32[256,256]{0,1:T(8,128)}) %reduce-scatter.2.cloned.1.call-update) | async-done | bytes 262160 | tf_op jit(solution)/shard_map/reduce_scatter | solution.py:89
  (73 shorter events, 18.2 us)
Async XLA Ops:
  7.2 64.7 %all-gather.2.cloned.1.call-start = ((), (), s32[]{:S(2)}) async-start(), calls=%async_computation.1 | async-start | bytes 2228224 | tf_op jit(solution)/shard_map/all_gather | solution.py:32
  8.3 0.6 copy-start.8
  9.6 235.4 %all-reduce.3.cloned.1.call-start = ((), (), s32[]{:S(2)}) async-start(), calls=%async_computation.3 | async-start | bytes 2097152
  9.6 94.5 %collective-permute-start = (bf16[256,4096]{1,0:T(8,128)(2,1)}, bf16[256,4096]{1,0:T(8,128)(2,1)}, u32[]{:S(2)}, u32[]{:S(2)}) collective-permute-start(bf16[256,4096]{1,0:T(8,128)(2,1)} %bitcast.85), channel_id=1, source_target_pairs={{0,1},{1,0},{2,3},{3,2},{4,5},{5,4},{6,7},{7,6},{8,9},{9,8},{10,11... | collective-permute-start | bytes 6291464 | tf_op jit(solution)/shard_map/ppermute | solution.py:13
  34.0 105.5 %collective-permute-start.1 = (f32[256,256]{1,0:T(8,128)}, f32[256,256]{1,0:T(8,128)}, u32[]{:S(2)}, u32[]{:S(2)}) collective-permute-start(f32[256,256]{1,0:T(8,128)} %bitcast_add_fusion), channel_id=1, source_target_pairs={{0,1},{1,0},{2,3},{3,2},{4,5},{5,4},{6,7},{7,6},{8,9},{9,8},{10,11... | collective-permute-start | bytes 786440 | tf_op jit(solution)/shard_map/ppermute | solution.py:13
  75.9 28.2 %copy-start.2 = (bf16[4096,256]{0,1:T(8,128)(2,1)S(1)}, bf16[4096,256]{0,1:T(8,128)(2,1)}, u32[]{:S(2)}) copy-start(bf16[4096,256]{0,1:T(8,128)(2,1)} %all-gather.2.cloned.1.call-done) | copy-start | bytes 6291460
  110.9 3.5 %copy-start.4 = (bf16[4096,256]{1,0:T(8,128)(2,1)S(1)}, bf16[4096,256]{1,0:T(8,128)(2,1)}, u32[]{:S(2)}) copy-start(bf16[4096,256]{1,0:T(8,128)(2,1)} %get-tuple-element.261) | copy-start | bytes 6291460 | tf_op jit(solution)/shard_map/while
  110.9 3.5 %copy-start.5 = (f32[2,512,256]{2,1,0:T(8,128)S(1)}, f32[2,512,256]{2,1,0:T(8,128)}, u32[]{:S(2)}) copy-start(f32[2,512,256]{2,1,0:T(8,128)} %get-tuple-element.250) | copy-start | bytes 3145732 | tf_op jit(solution)/shard_map/while
  114.4 2.2 copy-start
  116.6 1.8 copy-start.6
  118.4 1.9 copy-start.1
  120.4 3.5 %copy-start.4 = (bf16[4096,256]{1,0:T(8,128)(2,1)S(1)}, bf16[4096,256]{1,0:T(8,128)(2,1)}, u32[]{:S(2)}) copy-start(bf16[4096,256]{1,0:T(8,128)(2,1)} %get-tuple-element.261) | copy-start | bytes 6291460 | tf_op jit(solution)/shard_map/while
  120.4 3.5 %copy-start.5 = (f32[2,512,256]{2,1,0:T(8,128)S(1)}, f32[2,512,256]{2,1,0:T(8,128)}, u32[]{:S(2)}) copy-start(f32[2,512,256]{2,1,0:T(8,128)} %get-tuple-element.250) | copy-start | bytes 3145732 | tf_op jit(solution)/shard_map/while
  124.0 2.2 copy-start
  126.2 1.8 copy-start.6
  127.9 1.9 copy-start.1
  133.6 201.7 %reduce-scatter.2.cloned.1.call-start = ((), (), s32[]{:S(2)}) async-start(), calls=%async_computation.2 | async-start | bytes 4456448 | tf_op jit(solution)/shard_map/reduce_scatter | solution.py:89
  133.7 5.8 %copy-start.3 = (bf16[256,1,4096]{2,0,1:T(8,128)(2,1)S(1)}, bf16[256,1,4096]{2,0,1:T(8,128)(2,1)}, u32[]{:S(2)}) copy-start(bf16[256,1,4096]{2,0,1:T(8,128)(2,1)} %param.8) | copy-start | bytes 6291460
  144.5 0.7 copy-start.10
  144.5 100.5 %copy-start.7 = (bf16[16,1,4,256]{3,2,1,0:T(4,128)(2,1)S(1)}, bf16[16,1,4,256]{3,2,1,0:T(4,128)(2,1)}, u32[]{:S(2)}) copy-start(bf16[16,1,4,256]{3,2,1,0:T(4,128)(2,1)} %param.7) | copy-start | bytes 98308
  144.5 190.8 %copy-start.9 = (f32[256]{0:T(256)S(1)}, f32[256]{0:T(256)}, u32[]{:S(2)}) copy-start(f32[256]{0:T(256)} %copy-done.8) | copy-start | bytes 3076
Sparse Core Ops, SparseCore 0:
  10.9 60.8 all-gather.1
  133.7 111.2 all-reduce.2
  248.6 86.6 reduce-scatter.1
where the time goes:
time: 346 us; the launch traced here: 345 us
  waiting for transfers between devices  223 us (64%)
  blocking collectives  41.3 us (12%)
  matrix products  29.4 us (8%)
  local copies, waits for them, and re-layouts  22.6 us (7%)
  between operations  14.6 us (4%)
  other arithmetic  11.5 us (3%)
    unnamed x4, waiting for transfers between devices  98.7 us
    reduce_scatter x1, waiting for transfers between devices, on_device(): lax.psum_scatter(proto_sum, ('dp', 'crop'), scatter_dimension=0, tiled=True)  87.7 us
    all_gather x1, waiting for transfers between devices, on_device(): lax.all_gather(unit_proto.astype(jnp.bfloat16), ('dp', 'crop'), axis=0, t...  36.5 us
    psum x1, blocking collectives, on_device(): totals = lax.psum(partial_totals, 'proto')  22 us
    all_gather x1, blocking collectives, on_device(): gathered = lax.all_gather(rounded, 'proto', axis=0, tiled=True)  19.3 us
    dot_general x4, matrix products, block_exponent(): lax.dot_general(row_block, rescaled_input, (((1,), (1,)), ((), ())), pref...  13.1 us
    dot_general x3, matrix products, contract_first(): lax.dot_general(left, right, (((0,), (0,)), ((), ())), preferred_element_...  8.49 us
    unnamed x16, local copies, waits for them, and re-layouts  7.75 us
  transfers between devices with their start and end apart: 5, of which 3 were waited for; matrix products, arithmetic and copies ran while one was open for 15% of the time, Pallas kernels for 0%

commit v1 on v0

v1 whole, which is shorter than its diff:
```python
import jax
import jax.numpy as jnp
from jax import lax
from jax.sharding import PartitionSpec as P

sharpness = 10.0
epsilon = 1e-06
grad_scale = 8.0
f16, bf16, f32 = jnp.float16, jnp.bfloat16, jnp.float32


def swapped(value):
    return lax.ppermute(value, "crop", [(0, 1), (1, 0)])


def normalize_rows(values):
    floats = values.astype(f32)
    lengths = jnp.sqrt(jnp.sum(floats * floats, axis=-1, keepdims=True) + epsilon)
    return floats / lengths, lengths


def dot(left, right, dims):
    return lax.dot_general(left, right, ((dims[0], dims[1]), ((), ())), preferred_element_type=f32)


def on_device(embeddings, codes, prototypes):
    n_group = lax.axis_size(("dp", "crop"))
    n_proto = lax.axis_size("proto")
    crops = embeddings.shape[2]
    features = embeddings.shape[3]
    own_images = embeddings.shape[0]
    images = own_images * n_proto
    rows = images * crops
    own_rows = own_images * crops

    raw_proto = lax.all_to_all(
        jnp.broadcast_to(prototypes, (n_group, *prototypes.shape[1:])), ("dp", "crop"), 0, 0
    ).reshape(-1, features)
    raw_emb = lax.all_gather(embeddings.reshape(own_rows, features), "proto", axis=0, tiled=True)

    z = normalize_rows(raw_emb)[0].astype(bf16)
    c = normalize_rows(raw_proto)[0].astype(bf16)
    z_floats = z.astype(f32).reshape(images, crops, features)
    local_sum = jnp.sum(z_floats[:, 1:], axis=1)
    incoming = swapped(z_floats[:, 0] + local_sum)
    target_sum = (local_sum + incoming).astype(bf16)
    code = codes[:, 0]

    exponent = jnp.exp(dot(z, c, ((1,), (1,))) * sharpness)
    local_total = jnp.sum(exponent, axis=1, keepdims=True)
    exponent = exponent.astype(bf16)
    softened = dot(exponent, c, ((1,), (0,))) / local_total
    own_term = dot(code, c, ((1,), (0,)))
    log_total = jnp.log(local_total)
    log_high = log_total.astype(f16)
    log_low = (log_total - log_high.astype(f32)).astype(f16)
    log_pair = jnp.stack([log_high, log_low]).reshape(1, -1, features)
    payload = jnp.concatenate(
        [
            softened.astype(f16).reshape(n_proto, own_rows, features),
            own_term.astype(f16).reshape(n_proto, own_images, features),
            jnp.broadcast_to(log_pair, (n_proto, *log_pair.shape[1:])),
        ],
        axis=1,
    )
    received = lax.all_to_all(payload, "proto", 0, 0).astype(f32)
    logs = received[:, own_rows + own_images :].reshape(n_proto, 2, rows)
    totals_by_block = jnp.exp(logs[:, 0] + logs[:, 1])
    totals = jnp.sum(totals_by_block, axis=0)

    view_results = jnp.where(jnp.arange(crops) == 0, 1.0, 2.0).astype(f32)
    row_weight = jnp.tile(view_results, images)
    weighted = (z.astype(f32) * (row_weight / totals)[:, None]).astype(bf16)
    proto_sum = dot(exponent, weighted, ((0,), (0,))) - dot(code, target_sum, ((0,), (0,)))
    proto_parts = (proto_sum * grad_scale).astype(f16).reshape(n_group, -1, features)
    proto_parts = lax.all_to_all(proto_parts, ("dp", "crop"), 0, 0)

    first = lax.axis_index("proto") * own_rows
    own_share = lax.dynamic_slice_in_dim(
        totals_by_block * (row_weight / totals)[None, :], first, own_rows, 1
    )
    soft_rows = jnp.sum(received[:, :own_rows] * own_share[:, :, None], axis=0)
    soft_rows = soft_rows.reshape(own_images, crops, features)
    own_code_term = jnp.sum(received[:, own_rows : own_rows + own_images], axis=0)
    other_code_term = swapped(own_code_term)
    is_global = (jnp.arange(crops) == 0)[None, :, None]
    assigned = jnp.where(
        is_global, other_code_term[:, None], (own_code_term + other_code_term)[:, None]
    )
    unit_emb, emb_norm = normalize_rows(embeddings[:, 0])
    score_grad = (soft_rows - assigned) * sharpness
    grad_emb = (
        score_grad - unit_emb * jnp.sum(unit_emb * score_grad, axis=-1, keepdims=True)
    ) / emb_norm

    proto_grad = jnp.sum(proto_parts.astype(f32), axis=0) / grad_scale
    unit_proto, proto_norm = normalize_rows(prototypes[0])
    grad_proto = (
        proto_grad - unit_proto * jnp.sum(unit_proto * proto_grad, axis=-1, keepdims=True)
    ) / proto_norm
    return (grad_emb[:, None], grad_proto[None])


def solution(mesh):
    return jax.shard_map(
        on_device,
        mesh=mesh,
        in_specs=(
            P(("dp", "proto"), "crop", None, None),
            P("dp", "crop", "proto"),
            P("proto", ("dp", "crop"), None),
        ),
        out_specs=(P(("dp", "proto"), "crop", None, None), P("proto", ("dp", "crop"), None)),
        check_vma=False,
    )
```

time: 346 us -> 151 us (0.44)
  waiting for transfers between devices: 223 us -> 46.6 us
  blocking collectives: 41.3 us -> 19.3 us
  starting transfers between devices: 2.23 us -> 21.9 us
  other arithmetic: 11.5 us -> 26.3 us
  between operations: 14.6 us -> 0.91 us
  matrix products: 29.4 us -> 18.8 us
  local copies, waits for them, and re-layouts: 22.6 us -> 14.1 us
    unnamed x4 -> x0, waiting for transfers between devices: 98.7 us -> none
    reduce_scatter x1 -> x0, waiting for transfers between devices: 87.7 us -> none  [on_device(): lax.psum_scatter(proto_sum, ('dp', 'crop'), scatter_dimension=0, tiled=True)]
    all_gather x1 -> x0, waiting for transfers between devices: 36.5 us -> none  [on_device(): lax.all_gather(unit_proto.astype(jnp.bfloat16), ('dp', 'crop'), axis=0, t...]
    all_to_all x0 -> x3, waiting for transfers between devices: none -> 24.7 us  [the longest x1 12.4 us: on_device(): received = lax.all_to_all(payload, 'proto', 0, 0).astype(f32)]
    psum x1 -> x0, blocking collectives: 22 us -> none  [on_device(): totals = lax.psum(partial_totals, 'proto')]
    ppermute x2, waiting for transfers between devices: 0.01 us -> 21.8 us  [swapped(): return lax.ppermute(value, 'crop', [(0, 1), (1, 0)])]
    all_to_all x0 -> x3, starting transfers between devices: none -> 20.1 us  [the longest x1 8.59 us: on_device(): received = lax.all_to_all(payload, 'proto', 0, 0).astype(f32)]
    while x21 -> x0, local copies, waits for them, and re-layouts: 11.5 us -> none  [the longest x1 5.8 us: on_device(): lax.scan(backward_block, start_sum, (row_blocks, totals))]
  transfers between devices with their start and end apart: 5 -> 5, of which waited for: 3 -> 3; matrix products, arithmetic and copies ran while one was open for 15% -> 21% of each run, Pallas kernels for 0% -> 0%
where the time goes in v1:
time: 151 us; the launch traced here: 148 us
  waiting for transfers between devices  46.6 us (31%)
  other arithmetic  26.3 us (17%)
  starting transfers between devices  21.9 us (15%)
  blocking collectives  19.3 us (13%)
  matrix products  18.8 us (12%)
  local copies, waits for them, and re-layouts  14.1 us (9%)
    ppermute x2, waiting for transfers between devices, swapped(): return lax.ppermute(value, 'crop', [(0, 1), (1, 0)])  21.8 us
    all_gather x1, blocking collectives, on_device(): lax.all_gather(embeddings.reshape(own_rows, features), 'proto', axis=0, t...  19.3 us
    dot_general x5, matrix products, dot(): lax.dot_general(left, right, ((dims[0], dims[1]), ((), ())), preferred_el...  18.8 us
    all_to_all x1, waiting for transfers between devices, on_device(): received = lax.all_to_all(payload, 'proto', 0, 0).astype(f32)  12.4 us
    all_to_all x1, waiting for transfers between devices, on_device(): lax.all_to_all(jnp.broadcast_to(prototypes, (n_group, *prototypes.shape[1...  12.3 us
    all_to_all x1, starting transfers between devices, on_device(): received = lax.all_to_all(payload, 'proto', 0, 0).astype(f32)  8.59 us
    all_to_all x1, starting transfers between devices, on_device(): lax.all_to_all(jnp.broadcast_to(prototypes, (n_group, *prototypes.shape[1...  7.09 us
    unnamed x16, local copies, waits for them, and re-layouts  4.85 us
  transfers between devices with their start and end apart: 5, of which 3 were waited for; matrix products, arithmetic and copies ran while one was open for 21% of the time, Pallas kernels for 0%

profile of v1, /device:TPU:32, one launch (start us, length us, event | category | flops | bytes accessed | tf_op | source)
XLA Modules:
  0.0 147.8 jit_solution(1267659833959978761)
XLA Ops:
  0.7 2.6 %broadcast_in_dim.68 = bf16[16,256,256]{2,1,0:T(8,128)(2,1)} broadcast(bf16[256,256]{1,0:T(8,128)(2,1)} %bitcast.59), dimensions={1,2} | broadcast | bytes 2228224 | tf_op jit(solution)/shard_map/broadcast_in_dim | solution.py:37
  3.3 7.1 %all-to-all-start = ((bf16[16,256,256]{2,1,0:T(8,128)(2,1)}), bf16[16,256,256]{2,1,0:T(8,128)(2,1)}, u32[]{:S(2)}, u32[]{:S(2)}) async-start(bf16[16,256,256]{2,1,0:T(8,128)(2,1)} %broadcast_in_dim.68), calls=%async_computation | async-start | bytes 4194304 | tf_op jit(solution)/shard_map/all_to_all | solution.py:36
  10.4 19.3 %all_gather.3 = bf16[1024,256]{1,0:T(8,128)(2,1)S(1)} all-gather(bf16[64,256]{1,0:T(8,128)(2,1)S(1)} %reshape.177), channel_id=1, replica_groups=mesh['dp'=8,'proto'=16,'crop'=2] {'proto'}, dimensions={0}, use_global_device_ids=true | all-gather | bytes 557056 | tf_op jit(solution)/shard_map/all_gather | solution.py:39
  29.9 12.3 %all-to-all-done = bf16[16,256,256]{2,1,0:T(8,128)(2,1)} async-done(((bf16[16,256,256]{2,1,0:T(8,128)(2,1)}), bf16[16,256,256]{2,1,0:T(8,128)(2,1)}, u32[]{:S(2)}, u32[]{:S(2)}) %all-to-all-start) | async-done | bytes 2097184 | tf_op jit(solution)/shard_map/all_to_all | solution.py:36
  42.2 2.2 %multiply_reduce_fusion = f32[16,256]{1,0:T(8,128)S(1)} fusion(bf16[16,256,256]{2,1,0:T(8,128)(2,1)} %all-to-all-done), kind=kLoop, calls=%fused_computation.11 | loop fusion | flops 3141632 | bytes 2113536 | tf_op jit(solution)/shard_map/reduce_sum | solution.py:18
  44.4 2.0 %fusion.5 = bf16[4096,256]{1,0:T(8,128)(2,1)S(1)} fusion(bf16[16,256,256]{2,1,0:T(8,128)(2,1)} %all-to-all-done, f32[4096]{0:T(1024)S(1)} %bitcast.64), kind=kLoop, calls=%fused_computation.8 | loop fusion | flops 3145728 | bytes 4210688 | tf_op jit(solution)/shard_map/convert_element_type | solution.py:42
  46.4 3.1 %fusion = (f32[1024]{0:T(1024)S(1)}, f32[1024,4096]{1,0:T(8,128)S(1)}) fusion(bf16[4096,256]{1,0:T(8,128)(2,1)S(1)} %fusion.5, bf16[1024,256]{1,0:T(8,128)(2,1)S(1)} %all_gather.3, f32[1024]{0:T(1024)S(1)} %add_sqrt_fusion.2), kind=kOutput, calls=%fused_computation.1 | convolution fusion | flops 2156657664 | bytes 19406848 | tf_op jit(solution)/shard_map/dot_general | solution.py:23
  49.6 2.4 %divide_convert_fusion.1 = f16[1024,256]{1,0:T(8,128)(2,1)S(1)} fusion(bf16[4096,256]{1,0:T(8,128)(2,1)S(1)} %fusion.5, f32[1024,4096]{1,0:T(8,128)S(1)} %get-tuple-element.7, f32[1024]{0:T(1024)S(1)} %get-tuple-element.6), kind=kOutput, calls=%fused_computation.26 | convolution fusion | flops 2156396544 | bytes 19402752 | tf_op jit(solution)/shard_map/dot_general | solution.py:23
  52.0 3.3 %copy-done.6 = f32[1024,4096]{1,0:T(8,128)} copy-done((f32[1024,4096]{1,0:T(8,128)}, f32[1024,4096]{1,0:T(8,128)S(1)}, u32[]{:S(2)}) %copy-start.6) | copy-done | bytes 16777240
  55.3 1.9 %divide_convert_fusion = bf16[16,256,256]{2,1,0:T(8,128)(2,1)S(1)} fusion(bf16[16,256,256]{2,1,0:T(8,128)(2,1)} %all-to-all-done, f32[16,256]{1,0:T(8,128)S(1)} %get-tuple-element.4), kind=kLoop, calls=%fused_computation.10 | loop fusion | flops 3145728 | bytes 4210688 | tf_op jit(solution)/shard_map/convert_element_type | solution.py:42
  59.1 8.6 %all-to-all-start.1 = ((f16[16,88,256]{2,1,0:T(8,128)(2,1)}), f16[16,88,256]{2,1,0:T(8,128)(2,1)}, u32[]{:S(2)}, u32[]{:S(2)}) async-start(f16[16,88,256]{2,1,0:T(8,128)(2,1)} %pad_maximum_fusion), calls=%async_computation.1 | async-start | bytes 1441792 | tf_op jit(solution)/shard_map/all_to_all | solution.py:66
  68.9 1.5 %reshape.183 = f32[256,4,256]{2,1,0:T(4,128)S(1)} reshape(f32[1024,256]{1,0:T(8,128)} %fusion.40) | data formatting | bytes 2097152 | tf_op jit(solution)/shard_map/reshape | solution.py:43
  73.0 12.4 %all-to-all-done.1 = f16[16,88,256]{2,1,0:T(8,128)(2,1)} async-done(((f16[16,88,256]{2,1,0:T(8,128)(2,1)}), f16[16,88,256]{2,1,0:T(8,128)(2,1)}, u32[]{:S(2)}, u32[]{:S(2)}) %all-to-all-start.1) | async-done | bytes 720928 | tf_op jit(solution)/shard_map/all_to_all | solution.py:66
  85.4 1.2 convert_element_type.126
  87.3 1.6 %reshape.180 = f32[16,2,1024]{2,1,0:T(2,128)} reshape(f32[16,8,256]{2,1,0:T(8,128)} %slice.29) | data formatting | bytes 262144 | tf_op jit(solution)/shard_map/reshape | solution.py:67
  88.9 1.7 %fusion.43 = (f32[1024]{0:T(1024)S(1)}, f32[16,1,1024]{2,1,0:T(1,128)}) fusion(f32[16,2,1024]{2,1,0:T(2,128)} %reshape.180), kind=kLoop, calls=%fused_computation.67 | loop fusion | flops 31744 | bytes 200704 | tf_op jit(solution)/shard_map/reduce_sum | solution.py:69
  90.7 9.1 %fusion.6 = f32[4096,256]{1,0:T(8,128)S(1)} fusion(f32[1024,4096]{1,0:T(8,128)} %copy-done.6, f32[1024]{0:T(1024)S(1)} %div.97, bf16[1024,256]{1,0:T(8,128)(2,1)} %copy-done.1, f32[1024]{0:T(1024)S(1)} %add_sqrt_fusion.2), kind=kOutput, calls=%fused_computation.12 | convolution fusion | flops 2157445120 | bytes 21504000 | tf_op jit(solution)/shard_map/dot_general | solution.py:23
  99.9 3.4 %fusion.4 = f16[4096,256]{1,0:T(8,128)(2,1)} fusion(f32[4096,256]{1,0:T(8,128)S(1)} %fusion.6, bf16[256,1,4096]{2,0,1:T(8,128)(2,1)S(1)} %copy-done, f32[256,256]{1,0:T(8,128)S(1)} %copy-done.3, f32[256,256]{1,0:T(8,128)} %collective-permute-done.1), kind=kOutput, calls=%fused_computation.6 | convolution fusion | flops 540147712 | bytes 8912896 | tf_op jit(solution)/shard_map/dot_general | solution.py:23
  103.3 4.4 %all-to-all-start.2 = ((f16[16,256,256]{2,1,0:T(8,128)(2,1)}), f16[16,256,256]{2,1,0:T(8,128)(2,1)}, u32[]{:S(2)}, u32[]{:S(2)}) async-start(f16[16,256,256]{2,1,0:T(8,128)(2,1)} %bitcast.58), calls=%async_computation.2 | async-start | bytes 4194304 | tf_op jit(solution)/shard_map/all_to_all | solution.py:76
  112.0 1.7 %collective-permute-start = (f32[16,256]{1,0:T(8,128)}, f32[16,256]{1,0:T(8,128)S(1)}, u32[]{:S(2)}, u32[]{:S(2)}) collective-permute-start(f32[16,256]{1,0:T(8,128)} %slice_reduce_fusion.1), channel_id=1, source_target_pairs={{0,1},{1,0},{2,3},{3,2},{4,5},{5,4},{6,7},{7,6},{8,9},{9,8},{10,11... | collective-permute-start | bytes 49160 | tf_op jit(solution)/shard_map/ppermute | solution.py:13
  118.0 21.8 %collective-permute-done = f32[16,256]{1,0:T(8,128)S(1)} collective-permute-done((f32[16,256]{1,0:T(8,128)}, f32[16,256]{1,0:T(8,128)S(1)}, u32[]{:S(2)}, u32[]{:S(2)}) %collective-permute-start) | collective-permute-done | bytes 16416 | tf_op jit(solution)/shard_map/ppermute | solution.py:13
  141.5 1.5 %fusion.34 = f32[16,1,4,256]{3,2,1,0:T(4,128)} fusion(bf16[16,1,4,256]{3,2,1,0:T(4,128)(2,1)} %param.3, f32[16,1,4,256]{3,2,1,0:T(4,128)S(1)} %reshape.181, f32[16,4]{1,0:T(8,128)S(1)} %fusion.35, f32[16,4]{1,0:T(8,128)} %add_sqrt_fusion.1, f32[16,256]{1,0:T(8,128)S(1)} %add.68, f32[16,256]{1,0:T(8,128)S(1)} %collective-permute-done, ...), kind=kLoop, calls=%fused_computation.51 | loop fusion | flops 131072 | bytes 197124 | tf_op jit(solution)/shard_map/div | solution.py:92
  143.0 1.9 %convert_reduce_fusion = f32[256,256]{1,0:T(8,128)S(1)} fusion(f16[16,256,256]{2,1,0:T(8,128)(2,1)} %all-to-all-done.2), kind=kLoop, calls=%fused_computation.9 | loop fusion | flops 2031616 | bytes 2359296 | tf_op jit(solution)/shard_map/reduce_sum | solution.py:96
  146.1 1.8 %fusion.24 = f32[1,256,256]{2,1,0:T(8,128)} fusion(bf16[1,256,256]{2,1,0:T(8,128)(2,1)} %param.5, f32[256,256]{1,0:T(8,128)S(1)} %convert_reduce_fusion, f32[256]{0:T(256)S(1)} %fusion.26, f32[256]{0:T(256)} %add_sqrt_fusion.3), kind=kLoop, calls=%fused_computation.36 | loop fusion | flops 393216 | bytes 657408 | tf_op jit(solution)/shard_map/div | solution.py:98
  (53 shorter events, 17.8 us)
Async XLA Ops:
  0.6 56.6 %copy-start = (bf16[256,1,4096]{2,0,1:T(8,128)(2,1)S(1)}, bf16[256,1,4096]{2,0,1:T(8,128)(2,1)}, u32[]{:S(2)}) copy-start(bf16[256,1,4096]{2,0,1:T(8,128)(2,1)} %param.4) | copy-start | bytes 6291460
  0.6 9.7 %copy-start.4 = (bf16[16,1,4,256]{3,2,1,0:T(4,128)(2,1)S(1)}, bf16[16,1,4,256]{3,2,1,0:T(4,128)(2,1)}, u32[]{:S(2)}) copy-start(bf16[16,1,4,256]{3,2,1,0:T(4,128)(2,1)} %param.3) | copy-start | bytes 98308
  3.3 38.9 %all-to-all-start = ((bf16[16,256,256]{2,1,0:T(8,128)(2,1)}), bf16[16,256,256]{2,1,0:T(8,128)(2,1)}, u32[]{:S(2)}, u32[]{:S(2)}) async-start(bf16[16,256,256]{2,1,0:T(8,128)(2,1)} %broadcast_in_dim.68), calls=%async_computation | async-start | bytes 4194304 | tf_op jit(solution)/shard_map/all_to_all | solution.py:36
  29.7 38.0 %copy-start.1 = (bf16[1024,256]{1,0:T(8,128)(2,1)}, bf16[1024,256]{1,0:T(8,128)(2,1)S(1)}, u32[]{:S(2)}) copy-start(bf16[1024,256]{1,0:T(8,128)(2,1)S(1)} %all_gather.3) | copy-start | bytes 1572868
  49.6 5.7 %copy-start.6 = (f32[1024,4096]{1,0:T(8,128)}, f32[1024,4096]{1,0:T(8,128)S(1)}, u32[]{:S(2)}) copy-start(f32[1024,4096]{1,0:T(8,128)S(1)} %get-tuple-element.7) | copy-start | bytes 50331652
  59.1 26.3 %all-to-all-start.1 = ((f16[16,88,256]{2,1,0:T(8,128)(2,1)}), f16[16,88,256]{2,1,0:T(8,128)(2,1)}, u32[]{:S(2)}, u32[]{:S(2)}) async-start(f16[16,88,256]{2,1,0:T(8,128)(2,1)} %pad_maximum_fusion), calls=%async_computation.1 | async-start | bytes 1441792 | tf_op jit(solution)/shard_map/all_to_all | solution.py:66
  71.4 0.7 copy-start.2
  72.8 27.0 %collective-permute-start.1 = (f32[256,256]{1,0:T(8,128)}, f32[256,256]{1,0:T(8,128)}, u32[]{:S(2)}, u32[]{:S(2)}) collective-permute-start(f32[256,256]{1,0:T(8,128)} %bitcast_add_fusion), channel_id=1, source_target_pairs={{0,1},{1,0},{2,3},{3,2},{4,5},{5,4},{6,7},{7,6},{8,9},{9,8},{10,11... | collective-permute-start | bytes 786440 | tf_op jit(solution)/shard_map/ppermute | solution.py:13
  90.7 9.2 %copy-start.5 = (f32[1024]{0:T(1024)}, f32[1024]{0:T(1024)S(1)}, u32[]{:S(2)}) copy-start(f32[1024]{0:T(1024)S(1)} %div.97) | copy-start | bytes 12292
  90.7 9.2 %copy-start.3 = (f32[256,256]{1,0:T(8,128)S(1)}, f32[256,256]{1,0:T(8,128)}, u32[]{:S(2)}) copy-start(f32[256,256]{1,0:T(8,128)} %copy-done.2) | copy-start | bytes 786436
  103.3 39.7 %all-to-all-start.2 = ((f16[16,256,256]{2,1,0:T(8,128)(2,1)}), f16[16,256,256]{2,1,0:T(8,128)(2,1)}, u32[]{:S(2)}, u32[]{:S(2)}) async-start(f16[16,256,256]{2,1,0:T(8,128)(2,1)} %bitcast.58), calls=%async_computation.2 | async-start | bytes 4194304 | tf_op jit(solution)/shard_map/all_to_all | solution.py:76
  112.0 27.8 %collective-permute-start = (f32[16,256]{1,0:T(8,128)}, f32[16,256]{1,0:T(8,128)S(1)}, u32[]{:S(2)}, u32[]{:S(2)}) collective-permute-start(f32[16,256]{1,0:T(8,128)} %slice_reduce_fusion.1), channel_id=1, source_target_pairs={{0,1},{1,0},{2,3},{3,2},{4,5},{5,4},{6,7},{7,6},{8,9},{9,8},{10,11... | collective-permute-start | bytes 49160 | tf_op jit(solution)/shard_map/ppermute | solution.py:13
